TPU v7x, 32 devices: a whole 2x2x4 slice. The times are simulated.
32 devices in a mesh: dp: 2 (over x), expert: 16 (over z, y, core).
Axes of the slice: x: 2, y: 2, z: 4, core: 2. Of those that a mesh axis runs over, the one named last changes fastest.
Arguments:
- tokens: bfloat16 [4096, 2048], P(('dp', 'expert')), may hold values from -6 to 6
- cotangent: bfloat16 [4096, 2048], P(('dp', 'expert')), may hold values from -6 to 6
- expert_ids: int32 [4096, 8], P(('dp', 'expert')), may hold values from 0 to 127, as said below
- gate_probs: float32 [4096, 8], P(('dp', 'expert')), may hold values from 0.1 to 1
- gate_weight: bfloat16 [16, 2048, 128], P('expert'), may hold values from -0.125 to 0.125
- up_weight: bfloat16 [16, 2048, 128], P('expert'), may hold values from -0.125 to 0.125
- down_weight: bfloat16 [16, 128, 2048], P('expert'), may hold values from -0.1875 to 0.1875
Outputs:
- grad_input: bfloat16 [4096, 2048], P(('dp', 'expert'))
- grad_gate: bfloat16 [16, 2048, 128], P('expert')
- grad_up: bfloat16 [16, 2048, 128], P('expert')
- grad_down: bfloat16 [16, 128, 2048], P('expert')
Inputs may be any that keep to these rules, and one draw needn't show every extreme that they name: `expert_ids`: each row names 8 different experts. Among the 128 rows of one device, each window expert 0 to 1 is named by 1 to 8 rows, and in every draw one window expert of every device is named by exactly 8 rows.
All inputs are finite; a program needn't handle non-finite values.
Results may differ from a plain program's by a relative error of at most 0.0064.
Values may be sent and summed in bfloat16 or wider, within the bound.
No kernel may reach another device: no remote copies, remote signals or barrier semaphores. Data moves between devices by JAX's collectives and lax.ppermute only.
A program may use at most 64 MiB of HBM per device.

v0:
```python
import jax
import jax.numpy as jnp
from jax import lax
from jax.sharding import PartitionSpec as P

SLICES = 8
CAP = 8


def silu_parts(gate_pre):
    sigmoid_value = jax.nn.sigmoid(gate_pre)
    return (gate_pre * sigmoid_value, sigmoid_value * (1.0 + gate_pre * (1.0 - sigmoid_value)))


def expert_slice(rows_in, rows_cot, gate_rows, up_rows, down_rows):
    gate_pre = jnp.dot(rows_in, gate_rows, preferred_element_type=jnp.float32)
    upward = jnp.dot(rows_in, up_rows, preferred_element_type=jnp.float32)
    swish, slope = silu_parts(gate_pre)
    active = (swish * upward).astype(jnp.bfloat16)
    dhidden = lax.dot_general(
        rows_cot, down_rows, (((1,), (1,)), ((), ())), preferred_element_type=jnp.float32
    )
    dgate = (dhidden * upward * slope).astype(jnp.bfloat16)
    dupward = (dhidden * swish).astype(jnp.bfloat16)
    grad_down = lax.dot_general(
        active, rows_cot, (((0,), (0,)), ((), ())), preferred_element_type=jnp.float32
    )
    grad_gate = lax.dot_general(
        rows_in, dgate, (((0,), (0,)), ((), ())), preferred_element_type=jnp.float32
    )
    grad_up = lax.dot_general(
        rows_in, dupward, (((0,), (0,)), ((), ())), preferred_element_type=jnp.float32
    )
    partial_value = lax.dot_general(
        dgate, gate_rows, (((1,), (1,)), ((), ())), preferred_element_type=jnp.float32
    )
    partial_value = partial_value + lax.dot_general(
        dupward, up_rows, (((1,), (1,)), ((), ())), preferred_element_type=jnp.float32
    )
    return (partial_value, grad_gate, grad_up, grad_down)


def local(tokens, cotangent, expert_ids, gate_probs, gate_weight, up_weight, down_weight):
    devices = lax.axis_size("expert")
    window = devices // SLICES
    capacity = CAP
    width = tokens.shape[1]
    local_rows = tokens.shape[0]
    matched = expert_ids[:, :, None] == jnp.arange(window, dtype=jnp.int32)[None, None, :]
    hit_count = jnp.sum(matched.astype(jnp.int32), axis=1)
    chosen = jnp.sum(jnp.where(matched, gate_probs[:, :, None], 0.0), axis=1)
    slot_rank = jnp.cumsum(hit_count, axis=0) - hit_count
    placed = (hit_count[:, :, None] == 1) & (
        slot_rank[:, :, None] == jnp.arange(capacity, dtype=jnp.int32)[None, None, :]
    )
    picker = placed.astype(jnp.bfloat16)
    filled = jnp.any(placed, axis=0)
    owner_row = jnp.sum(
        jnp.where(placed, jnp.arange(local_rows, dtype=jnp.int32)[:, None, None], 0), axis=0
    )
    slot_prob = jnp.sum(jnp.where(placed, chosen[:, :, None], 0.0), axis=0)
    rows_in = jnp.einsum("tec,td->ecd", picker, tokens, preferred_element_type=jnp.float32).astype(
        jnp.bfloat16
    )
    picked_cot = jnp.einsum("tec,td->ecd", picker, cotangent, preferred_element_type=jnp.float32)
    rows_cot = (slot_prob[:, :, None] * picked_cot).astype(jnp.bfloat16)
    gate_rows = gate_weight[0]
    up_rows = up_weight[0]
    down_rows = down_weight[0]
    send_in = jnp.broadcast_to(rows_in[None], (SLICES, window, capacity, width)).reshape(
        devices, capacity, width
    )
    send_cot = jnp.broadcast_to(rows_cot[None], (SLICES, window, capacity, width)).reshape(
        devices, capacity, width
    )
    recv_in, recv_cot = (
        lax.all_to_all(send_in, "expert", split_axis=0, concat_axis=0, tiled=True),
        lax.all_to_all(send_cot, "expert", split_axis=0, concat_axis=0, tiled=True),
    )
    partial_value, grad_g, grad_u, grad_d = expert_slice(
        recv_in.reshape(devices * capacity, width),
        recv_cot.reshape(devices * capacity, width),
        gate_rows,
        up_rows,
        down_rows,
    )
    returned = lax.all_to_all(
        partial_value.astype(jnp.bfloat16).reshape(devices, capacity, width),
        "expert",
        split_axis=0,
        concat_axis=0,
        tiled=True,
    )
    back = jnp.sum(returned.reshape(SLICES, window, capacity, width).astype(jnp.float32), axis=0)
    summed_g, summed_u, summed_d = lax.psum((grad_g, grad_u, grad_d), "dp")
    kept = jnp.where(filled[:, :, None], back, jnp.float32(0)).reshape(window * capacity, width)
    grad_rows = (
        jnp.zeros((local_rows, width), jnp.float32)
        .at[owner_row.reshape(window * capacity)]
        .add(kept)
    )
    grad_input = grad_rows.astype(jnp.bfloat16)
    return (
        grad_input,
        summed_g.astype(jnp.bfloat16)[None],
        summed_u.astype(jnp.bfloat16)[None],
        summed_d.astype(jnp.bfloat16)[None],
    )


def solution(mesh):
    placed = (
        P(("dp", "expert"), None),
        P(("dp", "expert"), None),
        P(("dp", "expert"), None),
        P(("dp", "expert"), None),
        P("expert", None, None),
        P("expert", None, None),
        P("expert", None, None),
    )
    return jax.shard_map(
        local,
        mesh=mesh,
        in_specs=placed,
        out_specs=(
            P(("dp", "expert"), None),
            P("expert", None, None),
            P("expert", None, None),
            P("expert", None, None),
        ),
        check_vma=False,
    )
```

profile of v0, /device:TPU:0, one launch (start us, length us, event | category | flops | bytes accessed | tf_op | source)
XLA Modules:
  0.0 133.9 jit_solution(7606036372887287696)
XLA Ops:
  0.6 0.8 convert_reduce_fusion.1
  1.4 0.1 copy.19
  1.5 0.2 reduce_window_sum.11
  1.7 0.1 copy.21
  1.8 1.2 convolution_convert_fusion
  3.0 0.9 broadcast_in_dim.95
  3.9 7.5 %all-to-all-start.1 = ((bf16[16,8,2048]{2,1,0:T(8,128)(2,1)}), bf16[16,8,2048]{2,1,0:T(8,128)(2,1)S(1)}, u32[]{:S(2)}, u32[]{:S(2)}) async-start(bf16[16,8,2048]{2,1,0:T(8,128)(2,1)} %bitcast.6), calls=%async_computation.1 | async-start | bytes 1048576 | tf_op jit(solution)/shard_map/all_to_all | solution.py:77
  11.5 0.1 select_reduce_fusion
  11.6 0.2 fusion.2
  11.7 14.0 %all-to-all-done.1 = bf16[16,8,2048]{2,1,0:T(8,128)(2,1)S(1)} async-done(((bf16[16,8,2048]{2,1,0:T(8,128)(2,1)}), bf16[16,8,2048]{2,1,0:T(8,128)(2,1)S(1)}, u32[]{:S(2)}, u32[]{:S(2)}) %all-to-all-start.1) | async-done | bytes 524320 | tf_op jit(solution)/shard_map/all_to_all | solution.py:77
  25.7 0.8 broadcast_in_dim.94
  26.5 4.2 %all-to-all-start = ((bf16[16,8,2048]{2,1,0:T(8,128)(2,1)}), bf16[16,8,2048]{2,1,0:T(8,128)(2,1)S(1)}, u32[]{:S(2)}, u32[]{:S(2)}) async-start(bf16[16,8,2048]{2,1,0:T(8,128)(2,1)} %bitcast.2), calls=%async_computation | async-start | bytes 1048576 | tf_op jit(solution)/shard_map/all_to_all | solution.py:78
  30.7 0.1 fusion.32
  30.9 0.1 broadcast_in_dim.88
  30.9 0.2 select_reduce_fusion.2
  31.1 0.1 reshape.81
  31.2 0.3 fusion.5
  31.5 0.8 copy-done.1
  32.2 0.3 fusion.8
  32.6 12.4 %all-to-all-done = bf16[16,8,2048]{2,1,0:T(8,128)(2,1)S(1)} async-done(((bf16[16,8,2048]{2,1,0:T(8,128)(2,1)}), bf16[16,8,2048]{2,1,0:T(8,128)(2,1)S(1)}, u32[]{:S(2)}, u32[]{:S(2)}) %all-to-all-start) | async-done | bytes 524320 | tf_op jit(solution)/shard_map/all_to_all | solution.py:78
  45.0 1.3 %fusion.19 = f32[128,2048]{1,0:T(8,128)} fusion(bf16[16,8,2048]{2,1,0:T(8,128)(2,1)S(1)} %all-to-all-done, f32[128,128]{1,0:T(8,128)S(1)} %fusion.8, f32[128,128]{1,0:T(8,128)S(1)} %fusion.5), kind=kOutput, calls=%fused_computation.24 | convolution fusion | flops 67207168 | bytes 1703936 | tf_op jit(solution)/shard_map/dot_general | solution.py:25
  46.3 0.3 multiply_convert_fusion.1
  46.6 0.3 fusion.10
  47.0 0.3 fusion.3
  47.3 0.3 fusion.12
  47.6 0.7 copy-done.2
  48.3 1.1 fusion.1
  49.4 4.2 %all-to-all-start.2 = ((bf16[16,8,2048]{2,1,0:T(8,128)(2,1)}), bf16[16,8,2048]{2,1,0:T(8,128)(2,1)S(1)}, u32[]{:S(2)}, u32[]{:S(2)}) async-start(bf16[16,8,2048]{2,1,0:T(8,128)(2,1)} %fusion.1), calls=%async_computation.2 | async-start | bytes 1048576 | tf_op jit(solution)/shard_map/all_to_all | solution.py:87
  53.6 78.2 %all-reduce.2 = (bf16[2048,128]{1,0:T(8,128)(2,1)}, bf16[2048,128]{1,0:T(8,128)(2,1)}, bf16[128,2048]{1,0:T(8,128)(2,1)}) all-reduce(f32[2048,128]{1,0:T(8,128)S(1)} %fusion.12, f32[2048,128]{1,0:T(8,128)S(1)} %fusion.10, f32[128,2048]{1,0:T(8,128)} %fusion.19), channel_id=1, replica_groups=mesh['dp'=2,'expert'=16] {'dp'}, use_global_device_ids=true, to_apply=%region_8.9 | all-reduce | flops 786432 | bytes 4718592 | tf_op jit(solution)/shard_map/psum | solution.py:95
  131.8 0.1 convert_reduce_fusion
  131.9 1.1 scatter_custom_fusion
  133.0 0.9 convert_element_type.48
  (17 shorter events, 0.1 us)
Async XLA Ops:
  0.6 30.6 %copy-start = (bf16[1,2048,128]{2,1,0:T(8,128)(2,1)S(1)}, bf16[1,2048,128]{2,1,0:T(8,128)(2,1)}, u32[]{:S(2)}) copy-start(bf16[1,2048,128]{2,1,0:T(8,128)(2,1)} %param.11) | copy-start | bytes 1572868
  3.9 7.6 %copy-start.4 = (s32[128,8]{0,1:T(8,128)S(1)}, s32[128,8]{0,1:T(8,128)}, u32[]{:S(2)}) copy-start(s32[128,8]{0,1:T(8,128)} %param.9) | copy-start | bytes 12292
  3.9 7.6 %copy-start.5 = (f32[128,8]{0,1:T(8,128)S(1)}, f32[128,8]{0,1:T(8,128)}, u32[]{:S(2)}) copy-start(f32[128,8]{0,1:T(8,128)} %param.10) | copy-start | bytes 12292
  3.9 7.7 %copy-start.3 = (bf16[128,2048]{1,0:T(8,128)(2,1)S(1)}, bf16[128,2048]{1,0:T(8,128)(2,1)}, u32[]{:S(2)}) copy-start(bf16[128,2048]{1,0:T(8,128)(2,1)} %param.8) | copy-start | bytes 1572868
  3.9 21.8 %all-to-all-start.1 = ((bf16[16,8,2048]{2,1,0:T(8,128)(2,1)}), bf16[16,8,2048]{2,1,0:T(8,128)(2,1)S(1)}, u32[]{:S(2)}, u32[]{:S(2)}) async-start(bf16[16,8,2048]{2,1,0:T(8,128)(2,1)} %bitcast.6), calls=%async_computation.1 | async-start | bytes 1048576 | tf_op jit(solution)/shard_map/all_to_all | solution.py:77
  26.5 18.4 %all-to-all-start = ((bf16[16,8,2048]{2,1,0:T(8,128)(2,1)}), bf16[16,8,2048]{2,1,0:T(8,128)(2,1)S(1)}, u32[]{:S(2)}, u32[]{:S(2)}) async-start(bf16[16,8,2048]{2,1,0:T(8,128)(2,1)} %bitcast.2), calls=%async_computation | async-start | bytes 1048576 | tf_op jit(solution)/shard_map/all_to_all | solution.py:78
  31.2 1.1 copy-start.1
  32.5 13.8 %copy-start.6 = (bf16[1,128,2048]{2,1,0:T(8,128)(2,1)S(1)}, bf16[1,128,2048]{2,1,0:T(8,128)(2,1)}, u32[]{:S(2)}) copy-start(bf16[1,128,2048]{2,1,0:T(8,128)(2,1)} %param.13) | copy-start | bytes 1572868
  47.3 1.0 copy-start.2
  49.4 82.4 %all-to-all-start.2 = ((bf16[16,8,2048]{2,1,0:T(8,128)(2,1)}), bf16[16,8,2048]{2,1,0:T(8,128)(2,1)S(1)}, u32[]{:S(2)}, u32[]{:S(2)}) async-start(bf16[16,8,2048]{2,1,0:T(8,128)(2,1)} %fusion.1), calls=%async_computation.2 | async-start | bytes 1048576 | tf_op jit(solution)/shard_map/all_to_all | solution.py:87
where the time goes:
time: 135 us; the launch traced here: 134 us
  blocking collectives  78.2 us (58%)
  waiting for transfers between devices  26.4 us (20%)
  starting transfers between devices  15.9 us (12%)
  matrix products  5.7 us (4%)
  local copies, waits for them, and re-layouts  3.51 us (3%)
  other arithmetic  3.4 us (3%)
    psum x1, blocking collectives, local(): summed_g, summed_u, summed_d = lax.psum((grad_g, grad_u, grad_d), 'dp')  78.2 us
    all_to_all x1, waiting for transfers between devices, local(): lax.all_to_all(send_in, 'expert', split_axis=0, concat_axis=0, tiled=True)  14 us
    all_to_all x1, waiting for transfers between devices, local(): lax.all_to_all(send_cot, 'expert', split_axis=0, concat_axis=0, tiled=True)  12.4 us
    all_to_all x1, starting transfers between devices, local(): lax.all_to_all(send_in, 'expert', split_axis=0, concat_axis=0, tiled=True)  7.55 us
    all_to_all x1, starting transfers between devices, local(): lax.all_to_all(send_cot, 'expert', split_axis=0, concat_axis=0, tiled=True)  4.16 us
    all_to_all x1, starting transfers between devices, local(): lax.all_to_all(partial_value.astype(jnp.bfloat16).reshape(devices, capaci...  4.16 us
  transfers between devices with their start and end apart: 3, of which 2 were waited for; matrix products, arithmetic and copies ran while one was open for 1% of the time, Pallas kernels for 0%

commit v1 on v0

--- a/solution.py
+++ b/solution.py
@@ -5,6 +5,22 @@
 
 SLICES = 8
 CAP = 8
+
+
+def swapped_with_each(x, axis, split, join):
+    ways, here = (lax.axis_size(axis), lax.axis_index(axis))
+    width = x.shape[split] // ways
+    shape = list(x.shape)
+    shape[split] = width
+    height = shape[join]
+    shape[join] = height * ways
+    full = jnp.zeros(shape, x.dtype)
+    for mask in range(ways):
+        part = lax.dynamic_slice_in_dim(x, (here ^ mask) * width, width, axis=split)
+        if mask:
+            part = lax.ppermute(part, axis, [(d, d ^ mask) for d in range(ways)])
+        full = lax.dynamic_update_slice_in_dim(full, part, (here ^ mask) * height, axis=join)
+    return full
 
 
 def silu_parts(gate_pre):
@@ -75,7 +91,7 @@
     )
     recv_in, recv_cot = (
         lax.all_to_all(send_in, "expert", split_axis=0, concat_axis=0, tiled=True),
-        lax.all_to_all(send_cot, "expert", split_axis=0, concat_axis=0, tiled=True),
+        swapped_with_each(send_cot, "expert", 0, 0),
     )
     partial_value, grad_g, grad_u, grad_d = expert_slice(
         recv_in.reshape(devices * capacity, width),

time: 135 us -> 158 us (1.17)
  waiting for transfers between devices: 26.4 us -> 42.4 us
  starting transfers between devices: 15.9 us -> 23.4 us
    ppermute x0 -> x15, waiting for transfers between devices: none -> 42.4 us  [swapped_with_each(): part = lax.ppermute(part, axis, [(d, d ^ mask) for d in range(ways)])]
    all_to_all x1, waiting for transfers between devices: 14 us -> 0.01 us  [local(): lax.all_to_all(send_in, 'expert', split_axis=0, concat_axis=0, tiled=True)]
    all_to_all x1 -> x0, waiting for transfers between devices: 12.4 us -> none  [local(): lax.all_to_all(send_cot, 'expert', split_axis=0, concat_axis=0, tiled=True)]
    ppermute x0 -> x15, starting transfers between devices: none -> 12.1 us  [swapped_with_each(): part = lax.ppermute(part, axis, [(d, d ^ mask) for d in range(ways)])]
    all_to_all x1 -> x0, starting transfers between devices: 4.16 us -> none  [local(): lax.all_to_all(send_cot, 'expert', split_axis=0, concat_axis=0, tiled=True)]
  transfers between devices with their start and end apart: 3 -> 17, of which waited for: 2 -> 11; matrix products, arithmetic and copies ran while one was open for 1% -> 1% of each run, Pallas kernels for 0% -> 0%
where the time goes in v1:
time: 158 us
  blocking collectives  78.2 us (49%)
  waiting for transfers between devices  42.4 us (27%)
  starting transfers between devices  23.4 us (15%)
  matrix products  5.67 us (4%)
  local copies, waits for them, and re-layouts  3.61 us (2%)
  other arithmetic  3.4 us (2%)
    psum x1, blocking collectives, local(): summed_g, summed_u, summed_d = lax.psum((grad_g, grad_u, grad_d), 'dp')  78.2 us
    ppermute x15, waiting for transfers between devices, swapped_with_each(): part = lax.ppermute(part, axis, [(d, d ^ mask) for d in range(ways)])  42.4 us
    ppermute x15, starting transfers between devices, swapped_with_each(): part = lax.ppermute(part, axis, [(d, d ^ mask) for d in range(ways)])  12.1 us
    all_to_all x1, starting transfers between devices, local(): lax.all_to_all(send_in, 'expert', split_axis=0, concat_axis=0, tiled=True)  7.55 us
    all_to_all x1, starting transfers between devices, local(): lax.all_to_all(partial_value.astype(jnp.bfloat16).reshape(devices, capaci...  3.82 us
  transfers between devices with their start and end apart: 17, of which 11 were waited for; matrix products, arithmetic and copies ran while one was open for 1% of the time, Pallas kernels for 0%

profile of v1, /device:TPU:0, one launch (start us, length us, event | category | flops | bytes accessed | tf_op | source)
XLA Modules:
  0.0 157.7 jit_solution(628766871353325943)
XLA Ops:
  0.6 0.8 convert_reduce_fusion.1
  1.8 1.2 convolution_convert_fusion
  3.0 0.9 broadcast_in_dim.99
  3.9 7.5 %all-to-all-start = ((bf16[16,8,2048]{2,1,0:T(8,128)(2,1)}), bf16[16,8,2048]{2,1,0:T(8,128)(2,1)S(1)}, u32[]{:S(2)}, u32[]{:S(2)}) async-start(bf16[16,8,2048]{2,1,0:T(8,128)(2,1)} %bitcast.6), calls=%async_computation | async-start | bytes 1048576 | tf_op jit(solution)/shard_map/all_to_all | solution.py:93
  11.5 0.7 copy-done.5
  12.7 4.3 %collective-permute-start.14 = (bf16[1,8,2048]{2,1,0:T(8,128)(2,1)S(1)}, bf16[1,8,2048]{2,1,0:T(8,128)(2,1)S(1)}, u32[]{:S(2)}, u32[]{:S(2)}) collective-permute-start(bf16[1,8,2048]{2,1,0:T(8,128)(2,1)S(1)} %get-tuple-element.7), channel_id=1, source_target_pairs={{0,15},{1,14},{2,13},{3,12},{4,11},{5,10},{6,9},{7,8},{8,7},{9,6},... | collective-permute-start | bytes 98312 | tf_op jit(solution)/shard_map/ppermute | solution.py:21
  17.1 0.4 collective-permute-start.13
  17.5 3.2 %collective-permute-start.12 = (bf16[1,8,2048]{2,1,0:T(8,128)(2,1)S(1)}, bf16[1,8,2048]{2,1,0:T(8,128)(2,1)S(1)}, u32[]{:S(2)}, u32[]{:S(2)}) collective-permute-start(bf16[1,8,2048]{2,1,0:T(8,128)(2,1)S(1)} %get-tuple-element.9), channel_id=1, source_target_pairs={{0,13},{1,12},{2,15},{3,14},{4,9},{5,8},{6,11},{7,10},{8,5},{9,4},... | collective-permute-start | bytes 98312 | tf_op jit(solution)/shard_map/ppermute | solution.py:21
  21.6 0.5 collective-permute-done
  22.1 1.7 %collective-permute-start.1 = (bf16[1,8,2048]{2,1,0:T(8,128)(2,1)S(1)}, bf16[1,8,2048]{2,1,0:T(8,128)(2,1)S(1)}, u32[]{:S(2)}, u32[]{:S(2)}) collective-permute-start(bf16[1,8,2048]{2,1,0:T(8,128)(2,1)S(1)} %get-tuple-element.20), channel_id=1, source_target_pairs={{0,2},{1,3},{2,0},{3,1},{4,6},{5,7},{6,4},{7,5},{8,10},{9,11},{10,... | collective-permute-start | bytes 98312 | tf_op jit(solution)/shard_map/ppermute | solution.py:21
  23.9 3.7 %collective-permute-done.1 = bf16[1,8,2048]{2,1,0:T(8,128)(2,1)S(1)} collective-permute-done((bf16[1,8,2048]{2,1,0:T(8,128)(2,1)S(1)}, bf16[1,8,2048]{2,1,0:T(8,128)(2,1)S(1)}, u32[]{:S(2)}, u32[]{:S(2)}) %collective-permute-start.1) | collective-permute-done | bytes 32800 | tf_op jit(solution)/shard_map/ppermute | solution.py:21
  27.6 3.7 %collective-permute-done.2 = bf16[1,8,2048]{2,1,0:T(8,128)(2,1)S(1)} collective-permute-done((bf16[1,8,2048]{2,1,0:T(8,128)(2,1)S(1)}, bf16[1,8,2048]{2,1,0:T(8,128)(2,1)S(1)}, u32[]{:S(2)}, u32[]{:S(2)}) %collective-permute-start.2) | collective-permute-done | bytes 32800 | tf_op jit(solution)/shard_map/ppermute | solution.py:21
  31.3 3.9 %collective-permute-done.3 = bf16[1,8,2048]{2,1,0:T(8,128)(2,1)S(1)} collective-permute-done((bf16[1,8,2048]{2,1,0:T(8,128)(2,1)S(1)}, bf16[1,8,2048]{2,1,0:T(8,128)(2,1)S(1)}, u32[]{:S(2)}, u32[]{:S(2)}) %collective-permute-start.3) | collective-permute-done | bytes 32800 | tf_op jit(solution)/shard_map/ppermute | solution.py:21
  35.2 3.3 %collective-permute-done.4 = bf16[1,8,2048]{2,1,0:T(8,128)(2,1)S(1)} collective-permute-done((bf16[1,8,2048]{2,1,0:T(8,128)(2,1)S(1)}, bf16[1,8,2048]{2,1,0:T(8,128)(2,1)S(1)}, u32[]{:S(2)}, u32[]{:S(2)}) %collective-permute-start.4) | collective-permute-done | bytes 32800 | tf_op jit(solution)/shard_map/ppermute | solution.py:21
  38.6 4.8 %collective-permute-done.5 = bf16[1,8,2048]{2,1,0:T(8,128)(2,1)S(1)} collective-permute-done((bf16[1,8,2048]{2,1,0:T(8,128)(2,1)S(1)}, bf16[1,8,2048]{2,1,0:T(8,128)(2,1)S(1)}, u32[]{:S(2)}, u32[]{:S(2)}) %collective-permute-start.5) | collective-permute-done | bytes 32800 | tf_op jit(solution)/shard_map/ppermute | solution.py:21
  43.4 4.2 %collective-permute-done.6 = bf16[1,8,2048]{2,1,0:T(8,128)(2,1)S(1)} collective-permute-done((bf16[1,8,2048]{2,1,0:T(8,128)(2,1)S(1)}, bf16[1,8,2048]{2,1,0:T(8,128)(2,1)S(1)}, u32[]{:S(2)}, u32[]{:S(2)}) %collective-permute-start.6) | collective-permute-done | bytes 32800 | tf_op jit(solution)/shard_map/ppermute | solution.py:21
  47.6 0.7 collective-permute-start.7
  48.3 4.1 %collective-permute-done.7 = bf16[1,8,2048]{2,1,0:T(8,128)(2,1)S(1)} collective-permute-done((bf16[1,8,2048]{2,1,0:T(8,128)(2,1)S(1)}, bf16[1,8,2048]{2,1,0:T(8,128)(2,1)S(1)}, u32[]{:S(2)}, u32[]{:S(2)}) %collective-permute-start.7) | collective-permute-done | bytes 32800 | tf_op jit(solution)/shard_map/ppermute | solution.py:21
  52.4 4.4 %collective-permute-done.8 = bf16[1,8,2048]{2,1,0:T(8,128)(2,1)S(1)} collective-permute-done((bf16[1,8,2048]{2,1,0:T(8,128)(2,1)S(1)}, bf16[1,8,2048]{2,1,0:T(8,128)(2,1)S(1)}, u32[]{:S(2)}, u32[]{:S(2)}) %collective-permute-start.8) | collective-permute-done | bytes 32800 | tf_op jit(solution)/shard_map/ppermute | solution.py:21
  56.8 1.2 collective-permute-start.9
  58.0 4.5 %collective-permute-done.9 = bf16[1,8,2048]{2,1,0:T(8,128)(2,1)S(1)} collective-permute-done((bf16[1,8,2048]{2,1,0:T(8,128)(2,1)S(1)}, bf16[1,8,2048]{2,1,0:T(8,128)(2,1)S(1)}, u32[]{:S(2)}, u32[]{:S(2)}) %collective-permute-start.9) | collective-permute-done | bytes 32800 | tf_op jit(solution)/shard_map/ppermute | solution.py:21
  62.6 5.1 %collective-permute-done.10 = bf16[1,8,2048]{2,1,0:T(8,128)(2,1)S(1)} collective-permute-done((bf16[1,8,2048]{2,1,0:T(8,128)(2,1)S(1)}, bf16[1,8,2048]{2,1,0:T(8,128)(2,1)S(1)}, u32[]{:S(2)}, u32[]{:S(2)}) %collective-permute-start.10) | collective-permute-done | bytes 32800 | tf_op jit(solution)/shard_map/ppermute | solution.py:21
  68.1 0.7 copy-done.1
  69.2 1.3 fusion.19
  70.8 0.3 fusion.10
  71.4 0.3 fusion.12
  71.8 0.7 copy-done.2
  72.5 1.1 fusion.1
  73.6 3.8 %all-to-all-start.1 = ((bf16[16,8,2048]{2,1,0:T(8,128)(2,1)}), bf16[16,8,2048]{2,1,0:T(8,128)(2,1)S(1)}, u32[]{:S(2)}, u32[]{:S(2)}) async-start(bf16[16,8,2048]{2,1,0:T(8,128)(2,1)} %fusion.1), calls=%async_computation.1 | async-start | bytes 1048576 | tf_op jit(solution)/shard_map/all_to_all | solution.py:103
  77.4 78.2 %all-reduce.2 = (bf16[2048,128]{1,0:T(8,128)(2,1)}, bf16[2048,128]{1,0:T(8,128)(2,1)}, bf16[128,2048]{1,0:T(8,128)(2,1)}) all-reduce(f32[2048,128]{1,0:T(8,128)S(1)} %fusion.12, f32[2048,128]{1,0:T(8,128)S(1)} %fusion.10, f32[128,2048]{1,0:T(8,128)} %fusion.19), channel_id=1, replica_groups=mesh['dp'=2,'expert'=16] {'dp'}, use_global_device_ids=true, to_apply=%region_8.9 | all-reduce | flops 786432 | bytes 4718592 | tf_op jit(solution)/shard_map/psum | solution.py:111
  155.7 1.1 scatter_custom_fusion
  156.8 0.9 convert_element_type.48
  (62 shorter events, 3.3 us)
Async XLA Ops:
  0.6 67.2 %copy-start = (bf16[1,2048,128]{2,1,0:T(8,128)(2,1)S(1)}, bf16[1,2048,128]{2,1,0:T(8,128)(2,1)}, u32[]{:S(2)}) copy-start(bf16[1,2048,128]{2,1,0:T(8,128)(2,1)} %param.11) | copy-start | bytes 1572868
  3.9 8.4 %copy-start.3 = (bf16[128,2048]{1,0:T(8,128)(2,1)S(1)}, bf16[128,2048]{1,0:T(8,128)(2,1)}, u32[]{:S(2)}) copy-start(bf16[128,2048]{1,0:T(8,128)(2,1)} %param.8) | copy-start | bytes 1572868
  3.9 64.0 %all-to-all-start = ((bf16[16,8,2048]{2,1,0:T(8,128)(2,1)}), bf16[16,8,2048]{2,1,0:T(8,128)(2,1)S(1)}, u32[]{:S(2)}, u32[]{:S(2)}) async-start(bf16[16,8,2048]{2,1,0:T(8,128)(2,1)} %bitcast.6), calls=%async_computation | async-start | bytes 1048576 | tf_op jit(solution)/shard_map/all_to_all | solution.py:93
  11.5 0.7 copy-start.5
  11.5 0.7 copy-start.4
  12.7 55.0 %collective-permute-start.14 = (bf16[1,8,2048]{2,1,0:T(8,128)(2,1)S(1)}, bf16[1,8,2048]{2,1,0:T(8,128)(2,1)S(1)}, u32[]{:S(2)}, u32[]{:S(2)}) collective-permute-start(bf16[1,8,2048]{2,1,0:T(8,128)(2,1)S(1)} %get-tuple-element.7), channel_id=1, source_target_pairs={{0,15},{1,14},{2,13},{3,12},{4,11},{5,10},{6,9},{7,8},{8,7},{9,6},... | collective-permute-start | bytes 98312 | tf_op jit(solution)/shard_map/ppermute | solution.py:21
  17.1 50.7 %collective-permute-start.13 = (bf16[1,8,2048]{2,1,0:T(8,128)(2,1)S(1)}, bf16[1,8,2048]{2,1,0:T(8,128)(2,1)S(1)}, u32[]{:S(2)}, u32[]{:S(2)}) collective-permute-start(bf16[1,8,2048]{2,1,0:T(8,128)(2,1)S(1)} %get-tuple-element.8), channel_id=1, source_target_pairs={{0,14},{1,15},{2,12},{3,13},{4,10},{5,11},{6,8},{7,9},{8,6},{9,7},... | collective-permute-start | bytes 98312 | tf_op jit(solution)/shard_map/ppermute | solution.py:21
  17.5 50.3 %collective-permute-start.12 = (bf16[1,8,2048]{2,1,0:T(8,128)(2,1)S(1)}, bf16[1,8,2048]{2,1,0:T(8,128)(2,1)S(1)}, u32[]{:S(2)}, u32[]{:S(2)}) collective-permute-start(bf16[1,8,2048]{2,1,0:T(8,128)(2,1)S(1)} %get-tuple-element.9), channel_id=1, source_target_pairs={{0,13},{1,12},{2,15},{3,14},{4,9},{5,8},{6,11},{7,10},{8,5},{9,4},... | collective-permute-start | bytes 98312 | tf_op jit(solution)/shard_map/ppermute | solution.py:21
  20.6 47.1 %collective-permute-start.11 = (bf16[1,8,2048]{2,1,0:T(8,128)(2,1)S(1)}, bf16[1,8,2048]{2,1,0:T(8,128)(2,1)S(1)}, u32[]{:S(2)}, u32[]{:S(2)}) collective-permute-start(bf16[1,8,2048]{2,1,0:T(8,128)(2,1)S(1)} %get-tuple-element.10), channel_id=1, source_target_pairs={{0,12},{1,13},{2,14},{3,15},{4,8},{5,9},{6,10},{7,11},{8,4},{9,5},... | collective-permute-start | bytes 98312 | tf_op jit(solution)/shard_map/ppermute | solution.py:21
  20.9 1.2 collective-permute-start
  22.1 5.5 %collective-permute-start.1 = (bf16[1,8,2048]{2,1,0:T(8,128)(2,1)S(1)}, bf16[1,8,2048]{2,1,0:T(8,128)(2,1)S(1)}, u32[]{:S(2)}, u32[]{:S(2)}) collective-permute-start(bf16[1,8,2048]{2,1,0:T(8,128)(2,1)S(1)} %get-tuple-element.20), channel_id=1, source_target_pairs={{0,2},{1,3},{2,0},{3,1},{4,6},{5,7},{6,4},{7,5},{8,10},{9,11},{10,... | collective-permute-start | bytes 98312 | tf_op jit(solution)/shard_map/ppermute | solution.py:21
  27.6 3.7 %collective-permute-start.2 = (bf16[1,8,2048]{2,1,0:T(8,128)(2,1)S(1)}, bf16[1,8,2048]{2,1,0:T(8,128)(2,1)S(1)}, u32[]{:S(2)}, u32[]{:S(2)}) collective-permute-start(bf16[1,8,2048]{2,1,0:T(8,128)(2,1)S(1)} %get-tuple-element.19), channel_id=1, source_target_pairs={{0,3},{1,2},{2,1},{3,0},{4,7},{5,6},{6,5},{7,4},{8,11},{9,10},{10,... | collective-permute-start | bytes 98312 | tf_op jit(solution)/shard_map/ppermute | solution.py:21
  31.3 3.9 %collective-permute-start.3 = (bf16[1,8,2048]{2,1,0:T(8,128)(2,1)S(1)}, bf16[1,8,2048]{2,1,0:T(8,128)(2,1)S(1)}, u32[]{:S(2)}, u32[]{:S(2)}) collective-permute-start(bf16[1,8,2048]{2,1,0:T(8,128)(2,1)S(1)} %get-tuple-element.18), channel_id=1, source_target_pairs={{0,4},{1,5},{2,6},{3,7},{4,0},{5,1},{6,2},{7,3},{8,12},{9,13},{10,... | collective-permute-start | bytes 98312 | tf_op jit(solution)/shard_map/ppermute | solution.py:21
  35.2 3.3 %collective-permute-start.4 = (bf16[1,8,2048]{2,1,0:T(8,128)(2,1)S(1)}, bf16[1,8,2048]{2,1,0:T(8,128)(2,1)S(1)}, u32[]{:S(2)}, u32[]{:S(2)}) collective-permute-start(bf16[1,8,2048]{2,1,0:T(8,128)(2,1)S(1)} %get-tuple-element.17), channel_id=1, source_target_pairs={{0,5},{1,4},{2,7},{3,6},{4,1},{5,0},{6,3},{7,2},{8,13},{9,12},{10,... | collective-permute-start | bytes 98312 | tf_op jit(solution)/shard_map/ppermute | solution.py:21
  38.5 4.8 %collective-permute-start.5 = (bf16[1,8,2048]{2,1,0:T(8,128)(2,1)S(1)}, bf16[1,8,2048]{2,1,0:T(8,128)(2,1)S(1)}, u32[]{:S(2)}, u32[]{:S(2)}) collective-permute-start(bf16[1,8,2048]{2,1,0:T(8,128)(2,1)S(1)} %get-tuple-element.16), channel_id=1, source_target_pairs={{0,6},{1,7},{2,4},{3,5},{4,2},{5,3},{6,0},{7,1},{8,14},{9,15},{10,... | collective-permute-start | bytes 98312 | tf_op jit(solution)/shard_map/ppermute | solution.py:21
  43.3 4.2 %collective-permute-start.6 = (bf16[1,8,2048]{2,1,0:T(8,128)(2,1)S(1)}, bf16[1,8,2048]{2,1,0:T(8,128)(2,1)S(1)}, u32[]{:S(2)}, u32[]{:S(2)}) collective-permute-start(bf16[1,8,2048]{2,1,0:T(8,128)(2,1)S(1)} %get-tuple-element.15), channel_id=1, source_target_pairs={{0,7},{1,6},{2,5},{3,4},{4,3},{5,2},{6,1},{7,0},{8,15},{9,14},{10,... | collective-permute-start | bytes 98312 | tf_op jit(solution)/shard_map/ppermute | solution.py:21
  47.6 4.8 %collective-permute-start.7 = (bf16[1,8,2048]{2,1,0:T(8,128)(2,1)S(1)}, bf16[1,8,2048]{2,1,0:T(8,128)(2,1)S(1)}, u32[]{:S(2)}, u32[]{:S(2)}) collective-permute-start(bf16[1,8,2048]{2,1,0:T(8,128)(2,1)S(1)} %get-tuple-element.14), channel_id=1, source_target_pairs={{0,8},{1,9},{2,10},{3,11},{4,12},{5,13},{6,14},{7,15},{8,0},{9,1},... | collective-permute-start | bytes 98312 | tf_op jit(solution)/shard_map/ppermute | solution.py:21
  52.4 4.4 %collective-permute-start.8 = (bf16[1,8,2048]{2,1,0:T(8,128)(2,1)S(1)}, bf16[1,8,2048]{2,1,0:T(8,128)(2,1)S(1)}, u32[]{:S(2)}, u32[]{:S(2)}) collective-permute-start(bf16[1,8,2048]{2,1,0:T(8,128)(2,1)S(1)} %get-tuple-element.13), channel_id=1, source_target_pairs={{0,9},{1,8},{2,11},{3,10},{4,13},{5,12},{6,15},{7,14},{8,1},{9,0},... | collective-permute-start | bytes 98312 | tf_op jit(solution)/shard_map/ppermute | solution.py:21
  56.8 5.7 %collective-permute-start.9 = (bf16[1,8,2048]{2,1,0:T(8,128)(2,1)S(1)}, bf16[1,8,2048]{2,1,0:T(8,128)(2,1)S(1)}, u32[]{:S(2)}, u32[]{:S(2)}) collective-permute-start(bf16[1,8,2048]{2,1,0:T(8,128)(2,1)S(1)} %get-tuple-element.12), channel_id=1, source_target_pairs={{0,10},{1,11},{2,8},{3,9},{4,14},{5,15},{6,12},{7,13},{8,2},{9,3},... | collective-permute-start | bytes 98312 | tf_op jit(solution)/shard_map/ppermute | solution.py:21
  62.6 5.1 %collective-permute-start.10 = (bf16[1,8,2048]{2,1,0:T(8,128)(2,1)S(1)}, bf16[1,8,2048]{2,1,0:T(8,128)(2,1)S(1)}, u32[]{:S(2)}, u32[]{:S(2)}) collective-permute-start(bf16[1,8,2048]{2,1,0:T(8,128)(2,1)S(1)} %get-tuple-element.11), channel_id=1, source_target_pairs={{0,11},{1,10},{2,9},{3,8},{4,15},{5,14},{6,13},{7,12},{8,3},{9,2},... | collective-permute-start | bytes 98312 | tf_op jit(solution)/shard_map/ppermute | solution.py:21
  67.8 1.0 copy-start.1
  69.1 1.3 copy-start.6
  71.4 1.0 copy-start.2
  73.6 82.1 %all-to-all-start.1 = ((bf16[16,8,2048]{2,1,0:T(8,128)(2,1)}), bf16[16,8,2048]{2,1,0:T(8,128)(2,1)S(1)}, u32[]{:S(2)}, u32[]{:S(2)}) async-start(bf16[16,8,2048]{2,1,0:T(8,128)(2,1)} %fusion.1), calls=%async_computation.1 | async-start | bytes 1048576 | tf_op jit(solution)/shard_map/all_to_all | solution.py:103
